TPU v7x, 256 devices: a whole 4x4x8 slice. The times are simulated.
256 devices in a mesh: grp: 4 (over y), wide: 64 (over z, x, core).
Axes of the slice: x: 4, y: 4, z: 8, core: 2. Of those that a mesh axis runs over, the one named last changes fastest.
Arguments:
- tiles: bfloat16 [12288, 256, 256], P(('grp', 'wide')), may hold values from -0.59765625 to 0.59765625
- contraction: int32 [12288], P(('grp', 'wide')), may hold values from 0 to 15
- row_tile: int32 [12288], P(('grp', 'wide')), may hold values from 0 to 255, as said below
- owner_map: int32 [256], replicated, may hold values from 0 to 255, as said below
- panel: bfloat16 [4096, 768], P('grp'), may hold values from -0.5390625 to 0.5390625
Outputs:
- column_block: float32 [65536, 768], P('wide')
Inputs may be any that keep to these rules, and one draw needn't show every extreme that they name: `row_tile`: every row tile's owner is owner_map // 4; among the 48 contributions of one device at most 2 have row tiles of one owner, and on every device some owner gets exactly 2. `owner_map`: A permutation of the row tiles.
All inputs are finite; a program needn't handle non-finite values.
Results may differ from a plain program's by a relative error of at most 0.0003.
Values may be sent and summed in bfloat16 or wider, within the bound.
A program may use at most 192 MiB of HBM per device.

v0:
```python
import math
import jax
import jax.numpy as jnp
from jax import lax
from jax.sharding import PartitionSpec as P


def place_slots(row_ids, owner_map, out_dev):
    table_ids = jnp.arange(owner_map.shape[0], dtype=jnp.int32)
    position = jnp.sum(jnp.where(row_ids[..., None] == table_ids, owner_map, 0), axis=-1)
    target = position // out_dev
    serial = jnp.arange(row_ids.shape[-1], dtype=jnp.int32)
    earlier = (target[..., :, None] == target[..., None, :]) & (serial[:, None] > serial[None, :])
    ranking = jnp.sum(earlier.astype(jnp.int32), axis=-1)
    return (position % out_dev, target, ranking)


def add_products(summed, arrived, slot_labels, panel_tiles):
    slot_count = arrived.shape[0]
    block_rows = math.gcd(slot_count, 32)
    out_dev = summed.shape[0]
    local_ids = jnp.arange(out_dev, dtype=jnp.int32)

    def one_block(which_block, running, source_tiles, source_labels):
        part_tiles = lax.dynamic_slice_in_dim(source_tiles, which_block * block_rows, block_rows, 0)
        part_labels = lax.dynamic_slice_in_dim(
            source_labels, which_block * block_rows, block_rows, 0
        )
        chosen = jnp.take(panel_tiles, part_labels[:, 1], axis=0)
        products = jnp.einsum(
            "sab,sbc->sac", part_tiles, chosen, preferred_element_type=jnp.float32
        )
        row_hits = (part_labels[:, 0][:, None] == local_ids[None, :]).astype(jnp.float32)
        return running + jnp.einsum(
            "sr,sac->rac", row_hits, products, precision=lax.Precision.HIGHEST
        )

    return lax.fori_loop(
        0,
        slot_count // block_rows,
        lambda which_block, running: one_block(which_block, running, arrived, slot_labels),
        summed,
    )


def per_device(tiles, contraction, row_tile, owner_map, panel):
    wide_count = lax.axis_size("wide")
    tile_dev = tiles.shape[0]
    tile_side = tiles.shape[1]
    out_dev = owner_map.shape[0] // wide_count
    most_slots = tile_dev * 8 // (3 * wide_count)
    slot_total = wide_count * most_slots
    local_row, target, ranking = place_slots(row_tile, owner_map, out_dev)
    slot_index = target * most_slots + ranking
    outgoing = jnp.zeros((slot_total, tile_side, tile_side), tiles.dtype).at[slot_index].set(tiles)
    all_rows, all_contraction = (
        lax.all_gather(row_tile, "wide", axis=0, tiled=True),
        lax.all_gather(contraction, "wide", axis=0, tiled=True),
    )
    all_rows = all_rows.reshape(wide_count, tile_dev)
    all_contraction = all_contraction.reshape(wide_count, tile_dev)
    source_local, source_target, source_rank = place_slots(all_rows, owner_map, out_dev)
    source_ids = jnp.arange(wide_count, dtype=jnp.int32)
    mine = source_target == lax.axis_index("wide")
    arrive_index = jnp.where(mine, source_ids[:, None] * most_slots + source_rank, slot_total)
    label_pairs = jnp.stack([source_local, all_contraction], axis=-1).reshape(
        wide_count * tile_dev, 2
    )
    vacant_label = jnp.stack(
        [jnp.full((slot_total,), out_dev, jnp.int32), jnp.zeros((slot_total,), jnp.int32)], axis=1
    )
    arrived_labels = vacant_label.at[arrive_index.reshape(-1)].set(label_pairs, mode="drop")
    gathered = lax.all_gather(panel, "grp", axis=0, tiled=True)
    panel_tiles = gathered.reshape(gathered.shape[0] // tile_side, tile_side, gathered.shape[1])
    summed = jnp.zeros((out_dev, tile_side, gathered.shape[1]), jnp.float32)
    arrived = lax.all_to_all(outgoing, "wide", split_axis=0, concat_axis=0, tiled=True)
    summed = add_products(summed, arrived, arrived_labels, panel_tiles)
    summed = lax.psum(summed, "grp")
    return summed.reshape(out_dev * tile_side, gathered.shape[1])


def solution(mesh):
    return jax.shard_map(
        per_device,
        mesh=mesh,
        in_specs=(
            P(("grp", "wide"), None, None),
            P(("grp", "wide")),
            P(("grp", "wide")),
            P(),
            P("grp", None),
        ),
        out_specs=P("wide", None),
        check_vma=False,
    )
```

profile of v0, /device:TPU:1, one launch (start us, length us, event | category | flops | bytes accessed | tf_op | source)
XLA Modules:
  0.0 973.6 jit_solution(2914574177467141061)
XLA Ops:
  6.5 0.9 select_reduce_fusion.1
  7.4 0.2 convert_reduce_fusion.1
  7.6 5.9 broadcast_in_dim.68
  13.5 16.8 %scatter_fusion.1 = bf16[128,256,256]{2,1,0:T(8,128)(2,1)} fusion(bf16[128,256,256]{2,1,0:T(8,128)(2,1)} %broadcast_in_dim.68, s32[48]{0:T(128)S(1)} %fusion.19, bf16[48,256,256]{2,1,0:T(8,128)(2,1)} %param.7), kind=kCustom, calls=%fused_computation.2 | custom fusion | bytes 18874560 | tf_op jit(solution)/shard_map/scatter | solution.py:55
  30.4 13.3 %all-to-all-start = ((bf16[128,256,256]{2,1,0:T(8,128)(2,1)}), bf16[128,256,256]{2,1,0:T(8,128)(2,1)}, u32[]{:S(2)}, u32[]{:S(2)}) async-start(bf16[128,256,256]{2,1,0:T(8,128)(2,1)} %scatter_fusion.1), calls=%async_computation | async-start | bytes 33554432 | tf_op jit(solution)/shard_map/all_to_all | solution.py:76
  43.6 0.0 copy-start
  43.6 0.0 all-gather.2.cloned.1.call-start
  43.7 0.7 all-gather.2.cloned.1.call-update
  44.4 0.0 all-reduce.5.cloned.1.call-start
  44.5 0.0 copy-done.4
  44.5 0.6 dynamic-slice
  45.7 0.3 dynamic-update-slice
  46.0 0.3 dynamic-update-slice.1
  46.3 588.5 %all-reduce.2 = (s32[3072]{0:T(1024)S(1)}, s32[3072]{0:T(1024)S(1)}) all-reduce(s32[3072]{0:T(1024)S(1)} %dynamic-update-slice, s32[3072]{0:T(1024)S(1)} %dynamic-update-slice.1), channel_id=1, replica_groups=mesh['grp'=4,'wide'=64] {'wide'}, use_global_device_ids=true, to_apply=%add | all-reduce | flops 6144 | bytes 49152
  634.8 0.1 eq.107
  634.9 1.7 select_reduce_fusion
  636.6 0.1 reduce_sum.43
  636.7 0.1 copy.11
  636.8 0.5 convert_reduce_fusion
  637.3 0.1 copy.13
  637.4 0.1 add.152
  637.5 0.1 and_select_fusion
  637.6 1.7 copy.14
  639.3 0.0 copy-done
  639.3 8.5 scatter_fusion
  647.8 0.1 copy.15
  647.9 0.0 all-to-all-done
  647.9 231.6 %while.14 = (s32[]{:T(128)}, f32[4,256,768]{2,0,1:T(4,128)S(1)}, s32[128,2]{0,1:T(2,128)S(1)}, bf16[128,256,256]{2,1,0:T(8,128)(2,1)}, bf16[16,256,768]{2,1,0:T(...) while((s32[]{:T(128)}, f32[4,256,768]{2,0,1:T(4,128)S(1)}, ...), condition=%wide.region_7.8_spmd.clone, body=%wide.region_6.7_spmd.clone.sunk | while | flops 3531081216 | bytes 98572000 | solution.py:38
  648.1 0.1 constant_dynamic-slice_fusion.2
  648.2 9.4 gather_fusion
  657.5 17.7 %fusion.29 = f32[32,256,768]{2,1,0:T(8,128)} fusion(bf16[32,256,768]{2,1,0:T(8,128)(2,1)} %gather_fusion, pred[32]{0:T(512)(128)(4,1)S(1)} %and_bitcast_fusion.2, bf16[128,256,256]{2,1,0:T(8,128)(2,1)} %get-tuple-element.217, s32[]{:T(128)S(6)} %select_n.171), kind=kOutput, calls=%fused_computation.6.clone.1 | convolution fusion | flops 3227516928 | bytes 41943076 | tf_op jit(solution)/shard_map/while/body/eval_jaxpr/sab,sbc->sac/dot_general | solution.py:30
  675.2 30.7 %select_add_fusion.2 = f32[4,256,768]{2,0,1:T(4,128)S(1)} fusion(f32[4,256,768]{2,0,1:T(4,128)S(1)} %get-tuple-element.206, pred[]{:T(512)S(6)} %compare.49, f32[32,256,768]{2,1,0:T(8,128)} %fusion.29, s32[32]{0:T(128)S(1)} %get-tuple-element.195), kind=kOutput, calls=%fused_computation.11.clone.1 | convolution fusion | flops 303562880 | bytes 31457408 | tf_op jit(solution)/shard_map/while/body/eval_jaxpr/sr,sac->rac/dot_general | solution.py:34
  706.0 0.1 constant_dynamic-slice_fusion.2
  706.1 9.3 gather_fusion
  715.4 17.7 %fusion.29 = f32[32,256,768]{2,1,0:T(8,128)} fusion(bf16[32,256,768]{2,1,0:T(8,128)(2,1)} %gather_fusion, pred[32]{0:T(512)(128)(4,1)S(1)} %and_bitcast_fusion.2, bf16[128,256,256]{2,1,0:T(8,128)(2,1)} %get-tuple-element.217, s32[]{:T(128)S(6)} %select_n.171), kind=kOutput, calls=%fused_computation.6.clone.1 | convolution fusion | flops 3227516928 | bytes 41943076 | tf_op jit(solution)/shard_map/while/body/eval_jaxpr/sab,sbc->sac/dot_general | solution.py:30
  733.1 30.7 %select_add_fusion.2 = f32[4,256,768]{2,0,1:T(4,128)S(1)} fusion(f32[4,256,768]{2,0,1:T(4,128)S(1)} %get-tuple-element.206, pred[]{:T(512)S(6)} %compare.49, f32[32,256,768]{2,1,0:T(8,128)} %fusion.29, s32[32]{0:T(128)S(1)} %get-tuple-element.195), kind=kOutput, calls=%fused_computation.11.clone.1 | convolution fusion | flops 303562880 | bytes 31457408 | tf_op jit(solution)/shard_map/while/body/eval_jaxpr/sr,sac->rac/dot_general | solution.py:34
  763.8 0.1 constant_dynamic-slice_fusion.2
  763.9 9.3 gather_fusion
  773.2 17.7 %fusion.29 = f32[32,256,768]{2,1,0:T(8,128)} fusion(bf16[32,256,768]{2,1,0:T(8,128)(2,1)} %gather_fusion, pred[32]{0:T(512)(128)(4,1)S(1)} %and_bitcast_fusion.2, bf16[128,256,256]{2,1,0:T(8,128)(2,1)} %get-tuple-element.217, s32[]{:T(128)S(6)} %select_n.171), kind=kOutput, calls=%fused_computation.6.clone.1 | convolution fusion | flops 3227516928 | bytes 41943076 | tf_op jit(solution)/shard_map/while/body/eval_jaxpr/sab,sbc->sac/dot_general | solution.py:30
  790.9 30.7 %select_add_fusion.2 = f32[4,256,768]{2,0,1:T(4,128)S(1)} fusion(f32[4,256,768]{2,0,1:T(4,128)S(1)} %get-tuple-element.206, pred[]{:T(512)S(6)} %compare.49, f32[32,256,768]{2,1,0:T(8,128)} %fusion.29, s32[32]{0:T(128)S(1)} %get-tuple-element.195), kind=kOutput, calls=%fused_computation.11.clone.1 | convolution fusion | flops 303562880 | bytes 31457408 | tf_op jit(solution)/shard_map/while/body/eval_jaxpr/sr,sac->rac/dot_general | solution.py:34
  821.7 0.1 constant_dynamic-slice_fusion.2
  821.8 9.2 gather_fusion
  831.0 17.7 %fusion.29 = f32[32,256,768]{2,1,0:T(8,128)} fusion(bf16[32,256,768]{2,1,0:T(8,128)(2,1)} %gather_fusion, pred[32]{0:T(512)(128)(4,1)S(1)} %and_bitcast_fusion.2, bf16[128,256,256]{2,1,0:T(8,128)(2,1)} %get-tuple-element.217, s32[]{:T(128)S(6)} %select_n.171), kind=kOutput, calls=%fused_computation.6.clone.1 | convolution fusion | flops 3227516928 | bytes 41943076 | tf_op jit(solution)/shard_map/while/body/eval_jaxpr/sab,sbc->sac/dot_general | solution.py:30
  848.7 30.7 %select_add_fusion.2 = f32[4,256,768]{2,0,1:T(4,128)S(1)} fusion(f32[4,256,768]{2,0,1:T(4,128)S(1)} %get-tuple-element.206, pred[]{:T(512)S(6)} %compare.49, f32[32,256,768]{2,1,0:T(8,128)} %fusion.29, s32[32]{0:T(128)S(1)} %get-tuple-element.195), kind=kOutput, calls=%fused_computation.11.clone.1 | convolution fusion | flops 303562880 | bytes 31457408 | tf_op jit(solution)/shard_map/while/body/eval_jaxpr/sr,sac->rac/dot_general | solution.py:34
  879.5 2.2 copy.16
  881.7 0.0 all-reduce.5.cloned.1.call-update
  881.7 81.3 %all-reduce.5.cloned.1.call-done = f32[1024,768]{1,0:T(8,128)} async-done(((f32[1024,768]{1,0:T(8,128)}), f32[1024,768]{1,0:T(8,128)}) %all-reduce.5.cloned.1.call-update) | async-done | bytes 3145744 | tf_op jit(solution)/shard_map/psum | solution.py:78
  963.0 3.8 copy.38
  (30 shorter events, 0.2 us)
Async XLA Ops:
  30.4 14.1 %copy-start.4 = (u32[256]{0:T(256)S(1)}, u32[256]{0:T(256)}, u32[]{:S(2)}) copy-start(u32[256]{0:T(256)} %constant.118) | copy-start | bytes 3076
  30.4 15.4 %copy-start.2 = (s32[48]{0:T(128)S(1)}, s32[48]{0:T(128)}, u32[]{:S(2)}) copy-start(s32[48]{0:T(128)} %param.9) | copy-start | bytes 580
  30.4 15.6 %copy-start.3 = (s32[48]{0:T(128)S(1)}, s32[48]{0:T(128)}, u32[]{:S(2)}) copy-start(s32[48]{0:T(128)} %param.8) | copy-start | bytes 580
  30.4 604.5 %copy-start.1 = (s32[256]{0:T(256)S(1)}, s32[256]{0:T(256)}, u32[]{:S(2)}) copy-start(s32[256]{0:T(256)} %param.10) | copy-start | bytes 3076
  30.4 617.5 %all-to-all-start = ((bf16[128,256,256]{2,1,0:T(8,128)(2,1)}), bf16[128,256,256]{2,1,0:T(8,128)(2,1)}, u32[]{:S(2)}, u32[]{:S(2)}) async-start(bf16[128,256,256]{2,1,0:T(8,128)(2,1)} %scatter_fusion.1), calls=%async_computation | async-start | bytes 33554432 | tf_op jit(solution)/shard_map/all_to_all | solution.py:76
  43.6 595.7 %copy-start = (s32[128,2]{1,0:T(8,128)S(1)}, s32[128,2]{1,0:T(8,128)}, u32[]{:S(2)}) copy-start(s32[128,2]{1,0:T(8,128)} %constant.110.clone.1) | copy-start | bytes 3076
  43.6 604.2 %all-gather.2.cloned.1.call-start = ((), (), s32[]{:S(2)}) async-start(), calls=%async_computation.1 | async-start | bytes 7864320 | tf_op jit(solution)/shard_map/all_gather | solution.py:73
  44.4 918.6 %all-reduce.5.cloned.1.call-start = ((), (), s32[]{:S(2)}) async-start(), calls=%async_computation.2 | async-start | bytes 6291456 | tf_op jit(solution)/shard_map/psum | solution.py:78
Sparse Core Ops, SparseCore 0:
  46.3 69.3 all-gather.1
  881.9 81.1 all-reduce.4
where the time goes:
time: 974 us
  blocking collectives  589 us (60%)
  matrix products  194 us (20%)
  waiting for transfers between devices  82 us (8%)
  local copies, waits for them, and re-layouts  78 us (8%)
  between operations  14.2 us (1%)
  starting transfers between devices  13.3 us (1%)
    unnamed x1, blocking collectives  589 us
    dot_general x4, matrix products, one_block(): jnp.einsum('sr,sac->rac', row_hits, products, precision=lax.Precision.HIG...  123 us
    psum x1, waiting for transfers between devices, per_device(): summed = lax.psum(summed, 'grp')  81.3 us
    dot_general x4, matrix products, one_block(): jnp.einsum('sab,sbc->sac', part_tiles, chosen, preferred_element_type=jnp...  70.7 us
    gather x4, local copies, waits for them, and re-layouts, one_block(): chosen = jnp.take(panel_tiles, part_labels[:, 1], axis=0)  37.2 us
  transfers between devices with their start and end apart: 3, of which 1 were waited for; matrix products, arithmetic and copies ran while one was open for 1% of the time, Pallas kernels for 0%

commit v1 on v0

--- a/solution.py
+++ b/solution.py
@@ -75,7 +75,7 @@
     summed = jnp.zeros((out_dev, tile_side, gathered.shape[1]), jnp.float32)
     arrived = lax.all_to_all(outgoing, "wide", split_axis=0, concat_axis=0, tiled=True)
     summed = add_products(summed, arrived, arrived_labels, panel_tiles)
-    summed = lax.psum(summed, "grp")
+    summed = jnp.sum(lax.all_gather(summed, "grp"), axis=0)
     return summed.reshape(out_dev * tile_side, gathered.shape[1])
 
 

time: 974 us -> 1020 us (1.047)
  waiting for transfers between devices: 82 us -> 122 us
    all_gather x0 -> x1, waiting for transfers between devices: none -> 122 us  [per_device(): summed = jnp.sum(lax.all_gather(summed, 'grp'), axis=0)]
    psum x1 -> x0, waiting for transfers between devices: 81.3 us -> none  [per_device(): summed = lax.psum(summed, 'grp')]
where the time goes in v1:
time: 1020 us
  blocking collectives  589 us (58%)
  matrix products  194 us (19%)
  waiting for transfers between devices  122 us (12%)
  local copies, waits for them, and re-layouts  74.2 us (7%)
  between operations  14.2 us (1%)
  starting transfers between devices  13.3 us (1%)
  other arithmetic  11.1 us (1%)
    unnamed x1, blocking collectives  589 us
    dot_general x4, matrix products, one_block(): jnp.einsum('sr,sac->rac', row_hits, products, precision=lax.Precision.HIG...  123 us
    all_gather x1, waiting for transfers between devices, per_device(): summed = jnp.sum(lax.all_gather(summed, 'grp'), axis=0)  122 us
    dot_general x4, matrix products, one_block(): jnp.einsum('sab,sbc->sac', part_tiles, chosen, preferred_element_type=jnp...  70.7 us
    gather x4, local copies, waits for them, and re-layouts, one_block(): chosen = jnp.take(panel_tiles, part_labels[:, 1], axis=0)  37.2 us
  transfers between devices with their start and end apart: 3, of which 1 were waited for; matrix products, arithmetic and copies ran while one was open for 1% of the time, Pallas kernels for 0%

profile of v1, /device:TPU:1, one launch (start us, length us, event | category | flops | bytes accessed | tf_op | source)
XLA Modules:
  0.0 1017.7 jit_solution(15493608791800863690)
XLA Ops:
  6.5 0.9 select_reduce_fusion.1
  7.4 0.2 convert_reduce_fusion.1
  7.6 5.9 broadcast_in_dim.68
  13.5 16.8 %scatter_fusion.1 = bf16[128,256,256]{2,1,0:T(8,128)(2,1)} fusion(bf16[128,256,256]{2,1,0:T(8,128)(2,1)} %broadcast_in_dim.68, s32[48]{0:T(128)S(1)} %fusion.19, bf16[48,256,256]{2,1,0:T(8,128)(2,1)} %param.7), kind=kCustom, calls=%fused_computation.2 | custom fusion | bytes 18874560 | tf_op jit(solution)/shard_map/scatter | solution.py:55
  30.4 13.3 %all-to-all-start = ((bf16[128,256,256]{2,1,0:T(8,128)(2,1)}), bf16[128,256,256]{2,1,0:T(8,128)(2,1)}, u32[]{:S(2)}, u32[]{:S(2)}) async-start(bf16[128,256,256]{2,1,0:T(8,128)(2,1)} %scatter_fusion.1), calls=%async_computation | async-start | bytes 33554432 | tf_op jit(solution)/shard_map/all_to_all | solution.py:76
  43.6 0.0 copy-start
  43.6 0.0 all-gather.4.cloned.1.call-start
  43.7 0.7 all-gather.4.cloned.1.call-update
  44.4 0.0 all-gather.6.cloned.1.call-start
  44.5 0.0 copy-done.4
  44.5 0.6 dynamic-slice
  45.7 0.3 dynamic-update-slice
  46.0 0.3 dynamic-update-slice.1
  46.3 588.5 %all-reduce.2 = (s32[3072]{0:T(1024)S(1)}, s32[3072]{0:T(1024)S(1)}) all-reduce(s32[3072]{0:T(1024)S(1)} %dynamic-update-slice, s32[3072]{0:T(1024)S(1)} %dynamic-update-slice.1), channel_id=1, replica_groups=mesh['grp'=4,'wide'=64] {'wide'}, use_global_device_ids=true, to_apply=%add | all-reduce | flops 6144 | bytes 49152
  634.8 0.1 eq.107
  634.9 1.7 select_reduce_fusion
  636.6 0.1 reduce_sum.52
  636.7 0.1 copy.20
  636.8 0.5 convert_reduce_fusion
  637.3 0.1 copy.22
  637.4 0.1 add.150
  637.5 0.1 and_select_fusion
  637.6 1.7 copy.23
  639.3 0.0 copy-done
  639.3 8.5 scatter_fusion
  647.8 0.1 copy.24
  647.9 0.0 all-to-all-done
  647.9 231.6 %while.14 = (s32[]{:T(128)}, f32[4,256,768]{2,0,1:T(4,128)S(1)}, s32[128,2]{0,1:T(2,128)S(1)}, bf16[128,256,256]{2,1,0:T(8,128)(2,1)}, bf16[16,256,768]{2,1,0:T(...) while((s32[]{:T(128)}, f32[4,256,768]{2,0,1:T(4,128)S(1)}, ...), condition=%wide.region_7.8_spmd.clone, body=%wide.region_6.7_spmd.clone.sunk | while | flops 3531081216 | bytes 98572000 | solution.py:38
  648.1 0.1 constant_dynamic-slice_fusion.2
  648.2 9.4 gather_fusion
  657.5 17.7 %fusion.29 = f32[32,256,768]{2,1,0:T(8,128)} fusion(bf16[32,256,768]{2,1,0:T(8,128)(2,1)} %gather_fusion, pred[32]{0:T(512)(128)(4,1)S(1)} %and_bitcast_fusion.2, bf16[128,256,256]{2,1,0:T(8,128)(2,1)} %get-tuple-element.227, s32[]{:T(128)S(6)} %select_n.171), kind=kOutput, calls=%fused_computation.6.clone.1 | convolution fusion | flops 3227516928 | bytes 41943076 | tf_op jit(solution)/shard_map/while/body/eval_jaxpr/sab,sbc->sac/dot_general | solution.py:30
  675.2 30.7 %select_add_fusion.2 = f32[4,256,768]{2,0,1:T(4,128)S(1)} fusion(f32[4,256,768]{2,0,1:T(4,128)S(1)} %get-tuple-element.216, pred[]{:T(512)S(6)} %compare.49, f32[32,256,768]{2,1,0:T(8,128)} %fusion.29, s32[32]{0:T(128)S(1)} %get-tuple-element.205), kind=kOutput, calls=%fused_computation.11.clone.1 | convolution fusion | flops 303562880 | bytes 31457408 | tf_op jit(solution)/shard_map/while/body/eval_jaxpr/sr,sac->rac/dot_general | solution.py:34
  706.0 0.1 constant_dynamic-slice_fusion.2
  706.1 9.3 gather_fusion
  715.4 17.7 %fusion.29 = f32[32,256,768]{2,1,0:T(8,128)} fusion(bf16[32,256,768]{2,1,0:T(8,128)(2,1)} %gather_fusion, pred[32]{0:T(512)(128)(4,1)S(1)} %and_bitcast_fusion.2, bf16[128,256,256]{2,1,0:T(8,128)(2,1)} %get-tuple-element.227, s32[]{:T(128)S(6)} %select_n.171), kind=kOutput, calls=%fused_computation.6.clone.1 | convolution fusion | flops 3227516928 | bytes 41943076 | tf_op jit(solution)/shard_map/while/body/eval_jaxpr/sab,sbc->sac/dot_general | solution.py:30
  733.1 30.7 %select_add_fusion.2 = f32[4,256,768]{2,0,1:T(4,128)S(1)} fusion(f32[4,256,768]{2,0,1:T(4,128)S(1)} %get-tuple-element.216, pred[]{:T(512)S(6)} %compare.49, f32[32,256,768]{2,1,0:T(8,128)} %fusion.29, s32[32]{0:T(128)S(1)} %get-tuple-element.205), kind=kOutput, calls=%fused_computation.11.clone.1 | convolution fusion | flops 303562880 | bytes 31457408 | tf_op jit(solution)/shard_map/while/body/eval_jaxpr/sr,sac->rac/dot_general | solution.py:34
  763.8 0.1 constant_dynamic-slice_fusion.2
  763.9 9.3 gather_fusion
  773.2 17.7 %fusion.29 = f32[32,256,768]{2,1,0:T(8,128)} fusion(bf16[32,256,768]{2,1,0:T(8,128)(2,1)} %gather_fusion, pred[32]{0:T(512)(128)(4,1)S(1)} %and_bitcast_fusion.2, bf16[128,256,256]{2,1,0:T(8,128)(2,1)} %get-tuple-element.227, s32[]{:T(128)S(6)} %select_n.171), kind=kOutput, calls=%fused_computation.6.clone.1 | convolution fusion | flops 3227516928 | bytes 41943076 | tf_op jit(solution)/shard_map/while/body/eval_jaxpr/sab,sbc->sac/dot_general | solution.py:30
  790.9 30.7 %select_add_fusion.2 = f32[4,256,768]{2,0,1:T(4,128)S(1)} fusion(f32[4,256,768]{2,0,1:T(4,128)S(1)} %get-tuple-element.216, pred[]{:T(512)S(6)} %compare.49, f32[32,256,768]{2,1,0:T(8,128)} %fusion.29, s32[32]{0:T(128)S(1)} %get-tuple-element.205), kind=kOutput, calls=%fused_computation.11.clone.1 | convolution fusion | flops 303562880 | bytes 31457408 | tf_op jit(solution)/shard_map/while/body/eval_jaxpr/sr,sac->rac/dot_general | solution.py:34
  821.7 0.1 constant_dynamic-slice_fusion.2
  821.8 9.2 gather_fusion
  831.0 17.7 %fusion.29 = f32[32,256,768]{2,1,0:T(8,128)} fusion(bf16[32,256,768]{2,1,0:T(8,128)(2,1)} %gather_fusion, pred[32]{0:T(512)(128)(4,1)S(1)} %and_bitcast_fusion.2, bf16[128,256,256]{2,1,0:T(8,128)(2,1)} %get-tuple-element.227, s32[]{:T(128)S(6)} %select_n.171), kind=kOutput, calls=%fused_computation.6.clone.1 | convolution fusion | flops 3227516928 | bytes 41943076 | tf_op jit(solution)/shard_map/while/body/eval_jaxpr/sab,sbc->sac/dot_general | solution.py:30
  848.7 30.7 %select_add_fusion.2 = f32[4,256,768]{2,0,1:T(4,128)S(1)} fusion(f32[4,256,768]{2,0,1:T(4,128)S(1)} %get-tuple-element.216, pred[]{:T(512)S(6)} %compare.49, f32[32,256,768]{2,1,0:T(8,128)} %fusion.29, s32[32]{0:T(128)S(1)} %get-tuple-element.205), kind=kOutput, calls=%fused_computation.11.clone.1 | convolution fusion | flops 303562880 | bytes 31457408 | tf_op jit(solution)/shard_map/while/body/eval_jaxpr/sr,sac->rac/dot_general | solution.py:34
  879.5 2.2 copy.25
  881.7 0.0 all-gather.6.cloned.1.call-update
  881.7 121.5 %all-gather.6.cloned.1.call-done = f32[16,256,768]{2,1,0:T(8,128)} async-done(((f32[4,256,768]{2,1,0:T(8,128)}), f32[16,256,768]{2,1,0:T(8,128)}) %all-gather.6.cloned.1.call-update) | async-done | bytes 12582928 | tf_op jit(solution)/shard_map/all_gather | solution.py:78
  1003.3 7.6 reduce_sum.58
  (30 shorter events, 0.2 us)
Async XLA Ops:
  30.4 14.1 %copy-start.4 = (u32[256]{0:T(256)S(1)}, u32[256]{0:T(256)}, u32[]{:S(2)}) copy-start(u32[256]{0:T(256)} %constant.119) | copy-start | bytes 3076
  30.4 15.4 %copy-start.2 = (s32[48]{0:T(128)S(1)}, s32[48]{0:T(128)}, u32[]{:S(2)}) copy-start(s32[48]{0:T(128)} %param.9) | copy-start | bytes 580
  30.4 15.6 %copy-start.3 = (s32[48]{0:T(128)S(1)}, s32[48]{0:T(128)}, u32[]{:S(2)}) copy-start(s32[48]{0:T(128)} %param.8) | copy-start | bytes 580
  30.4 604.5 %copy-start.1 = (s32[256]{0:T(256)S(1)}, s32[256]{0:T(256)}, u32[]{:S(2)}) copy-start(s32[256]{0:T(256)} %param.10) | copy-start | bytes 3076
  30.4 617.5 %all-to-all-start = ((bf16[128,256,256]{2,1,0:T(8,128)(2,1)}), bf16[128,256,256]{2,1,0:T(8,128)(2,1)}, u32[]{:S(2)}, u32[]{:S(2)}) async-start(bf16[128,256,256]{2,1,0:T(8,128)(2,1)} %scatter_fusion.1), calls=%async_computation | async-start | bytes 33554432 | tf_op jit(solution)/shard_map/all_to_all | solution.py:76
  43.6 595.7 %copy-start = (s32[128,2]{1,0:T(8,128)S(1)}, s32[128,2]{1,0:T(8,128)}, u32[]{:S(2)}) copy-start(s32[128,2]{1,0:T(8,128)} %constant.111.clone.1) | copy-start | bytes 3076
  43.6 604.2 %all-gather.4.cloned.1.call-start = ((), (), s32[]{:S(2)}) async-start(), calls=%async_computation.1 | async-start | bytes 7864320 | tf_op jit(solution)/shard_map/all_gather | solution.py:73
  44.4 958.9 %all-gather.6.cloned.1.call-start = ((), (), s32[]{:S(2)}) async-start(), calls=%async_computation.2 | async-start | bytes 15728640 | tf_op jit(solution)/shard_map/all_gather | solution.py:78
Sparse Core Ops, SparseCore 0:
  46.3 69.3 all-gather.3
  881.9 121.3 all-gather.5
